TPU v7x, 512 devices: a whole 4x8x8 slice. The times are simulated.
512 devices in a mesh: pts: 128 (over z, y, core), ch: 4 (over x).
Axes of the slice: x: 4, y: 8, z: 8, core: 2. Of those that a mesh axis runs over, the one named last changes fastest.
Arguments:
- points_in: bfloat16 [65536, 256], P('pts'), may hold values from -6 to 6
- neighbor_offsets: int32 [65536, 16], P('pts'), may hold values from -128 to 128, as said below
- kernel_ids: int32 [65536, 16], P('pts'), may hold values from 0 to 26
- cluster_ids: int32 [65536], P('pts'), may hold values from 0 to 16383, as said below
- owners: int32 [65536], P('pts'), may hold values from 0 to 127, as said below
- conv_weight: bfloat16 [27, 256], replicated, may hold values from -1.5 to 1.5
- norm_gain: float32 [256], replicated, may hold values from 0.1 to 1.9
- norm_bias: float32 [256], replicated, may hold values from -3 to 3
- qkv_weight: bfloat16 [3, 256, 256], P(None, None, 'ch'), may hold values from -20 to 20
- proj_weight: bfloat16 [256, 256], replicated, may hold values from -1.5 to 1.5
- pool_weight: bfloat16 [256, 512], P(None, 'ch'), may hold values from -0.375 to 0.375
Outputs:
- block_out: bfloat16 [65536, 256], P('pts', 'ch')
- pooled: bfloat16 [16384, 512], P('pts', 'ch')
Inputs may be any that keep to these rules, and one draw needn't show every extreme that they name: `owners`: each device's points name every owner at most 8 times; in every draw one owner is named exactly 8 times by the points of every device. `cluster_ids`: cluster ids never fall along the points, every cluster holds one or more points, the points of device i belong to clusters i * 128 - 1 .. i * 128 + 127, and only the first 1 to 3 points of a device (none on device 0) lie in cluster i * 128 - 1; some device has exactly 3 such points. `neighbor_offsets`: offsets -128 and 128 both occur.
All inputs are finite; a program needn't handle non-finite values.
Results may differ from a plain program's by a relative error of at most 0.017.
Values may be sent and summed in bfloat16 or wider, within the bound.
No kernel may reach another device: no remote copies, remote signals or barrier semaphores. Data moves between devices by JAX's collectives and lax.ppermute only.
A program may use at most 64 MiB of HBM per device.

v0:
```python
import math
import jax
import jax.numpy as jnp
from jax import lax
from jax.sharding import PartitionSpec as P

HD = 32
PATCH = 1024
G = 128


def padded_2(value, sides, width):
    for axis, dim in sides:
        devices, length = (lax.axis_size(axis), value.shape[dim])
        up = [(i, (i + 1) % devices) for i in range(devices - 1)]
        down = [(j, i) for i, j in up]
        last = lax.slice_in_dim(value, length - width, length, axis=dim)
        initial = lax.slice_in_dim(value, 0, width, axis=dim)
        before = lax.ppermute(last, axis, up)
        after = lax.ppermute(initial, axis, down)
        value = jnp.concatenate([before, value, after], axis=dim)
    return value


def from_behind(value, axis, by):
    devices = lax.axis_size(axis)
    pairs = [(i, i + by) for i in range(devices) if 0 <= i + by < devices]
    return lax.ppermute(value, axis, pairs)


def attend_patches(packed_rows, live_slots, heads_here):
    slot_total = packed_rows.shape[0]
    patch_count = slot_total // PATCH
    head_cols = packed_rows.shape[1] // 3
    head_size = head_cols // heads_here
    score_scale = 1.0 / math.sqrt(head_size)
    patch_cube = packed_rows.reshape(patch_count, PATCH, 3, heads_here, head_size)
    key_alive = live_slots.reshape(patch_count, PATCH)

    def one_patch(operands):
        patch_rows, alive_keys = operands
        queries = patch_rows[:, 0]
        key_rows = patch_rows[:, 1]
        value_rows = patch_rows[:, 2]
        scores = (
            jnp.einsum("qhd,khd->hqk", queries, key_rows, preferred_element_type=jnp.float32)
            * score_scale
        )
        scores = jnp.where(alive_keys[None, None, :], scores, -1e30)
        row_max = jnp.max(scores, axis=-1, keepdims=True)
        exponent = jnp.exp(scores - row_max)
        denominator = jnp.sum(exponent, axis=-1)
        summed = jnp.einsum(
            "hqk,khd->qhd",
            exponent.astype(jnp.bfloat16),
            value_rows,
            preferred_element_type=jnp.float32,
        )
        return (summed / jnp.transpose(denominator)[:, :, None]).astype(jnp.bfloat16)

    attended = lax.map(one_patch, (patch_cube, key_alive))
    return attended.reshape(slot_total, head_cols)


def shards(
    points_in,
    neighbor_offsets,
    kernel_ids,
    cluster_ids,
    owners,
    conv_weight,
    norm_gain,
    norm_bias,
    qkv_weight,
    proj_weight,
    pool_weight,
):
    point_rows = points_in.shape[0]
    feature_count = points_in.shape[1]
    node_count = lax.axis_size("pts")
    my_index = lax.axis_index("pts")
    channel_index = lax.axis_index("ch")
    capacity = 2 * point_rows // node_count
    slot_total = capacity * node_count
    head_cols = qkv_weight.shape[2]
    heads_here = head_cols // HD
    padded = padded_2(points_in, (("pts", 0),), G)
    offsets_base = jnp.arange(point_rows, dtype=jnp.int32) + G
    kind_ids = jnp.arange(conv_weight.shape[0], dtype=jnp.int32)
    conv = jnp.zeros((point_rows, feature_count), jnp.float32)
    for neighbor_slot in range(neighbor_offsets.shape[1]):
        selector = (kernel_ids[:, neighbor_slot][:, None] == kind_ids[None, :]).astype(jnp.bfloat16)
        weights_here = jnp.dot(selector, conv_weight, preferred_element_type=jnp.float32)
        picked = padded[offsets_base + neighbor_offsets[:, neighbor_slot]]
        conv = conv + weights_here * picked.astype(jnp.float32)
    residual_rows = (points_in.astype(jnp.float32) + conv).astype(jnp.bfloat16)
    features = residual_rows.astype(jnp.float32)
    average = jnp.mean(features, axis=1, keepdims=True)
    centered = features - average
    variance = jnp.mean(centered * centered, axis=1, keepdims=True)
    normed_rows = (centered / jnp.sqrt(variance + 1e-05) * norm_gain + norm_bias).astype(
        jnp.bfloat16
    )
    flat_weight = jnp.transpose(qkv_weight, (1, 0, 2)).reshape(feature_count, 3 * head_cols)
    peer_ids = jnp.arange(node_count, dtype=jnp.int32)
    dest_marks = (owners[:, None] == peer_ids[None, :]).astype(jnp.int32)
    earlier_count = jnp.cumsum(dest_marks, axis=0) - dest_marks
    slot_index = jnp.sum(earlier_count * dest_marks, axis=1)
    send_counts = jnp.sum(dest_marks, axis=0).reshape(node_count, 1)
    position = owners * capacity + slot_index
    projected = jnp.dot(normed_rows, flat_weight, preferred_element_type=jnp.float32).astype(
        jnp.bfloat16
    )
    outgoing = (
        jnp.zeros((slot_total, projected.shape[1]), projected.dtype)
        .at[position]
        .set(projected)
        .reshape(node_count, capacity * 3 * head_cols)
    )
    arrived, incoming_counts = (
        lax.all_to_all(outgoing, "pts", split_axis=0, concat_axis=0, tiled=True),
        lax.all_to_all(send_counts, "pts", split_axis=0, concat_axis=0, tiled=True),
    )
    packed_rows = arrived.reshape(slot_total, 3 * head_cols)
    live_slots = (jnp.arange(capacity, dtype=jnp.int32)[None, :] < incoming_counts).reshape(
        slot_total
    )
    attended = attend_patches(packed_rows, live_slots, heads_here)
    returned_rows = lax.all_to_all(
        attended.reshape(node_count, capacity * head_cols),
        "pts",
        split_axis=0,
        concat_axis=0,
        tiled=True,
    )
    returned = returned_rows.reshape(slot_total, head_cols)[position]
    projected_sum = jnp.dot(
        lax.all_gather(returned, "ch", axis=1, tiled=True),
        proj_weight,
        preferred_element_type=jnp.float32,
    )
    full_out = (residual_rows.astype(jnp.float32) + projected_sum).astype(jnp.bfloat16)
    block_out = lax.dynamic_slice_in_dim(full_out, channel_index * head_cols, head_cols, 1)
    lifted_rows = jnp.dot(full_out, pool_weight, preferred_element_type=jnp.float32)
    cluster_count = point_rows // 4
    local_cluster = cluster_ids - my_index * cluster_count + 1
    cluster_sums = jax.ops.segment_sum(lifted_rows, local_cluster, num_segments=cluster_count + 1)
    point_counts = jax.ops.segment_sum(
        jnp.ones((point_rows,), jnp.float32), local_cluster, num_segments=cluster_count + 1
    )
    spill_sum, spill_count = from_behind((cluster_sums[:1], point_counts[:1]), "pts", -1)
    own_sums = cluster_sums[1:].at[cluster_count - 1].add(spill_sum[0])
    own_counts = point_counts[1:].at[cluster_count - 1].add(spill_count[0])
    pooled = jax.nn.gelu(own_sums / own_counts[:, None], approximate=False).astype(jnp.bfloat16)
    return (block_out, pooled)


def solution(mesh):
    return jax.shard_map(
        shards,
        mesh=mesh,
        in_specs=(
            P("pts", None),
            P("pts", None),
            P("pts", None),
            P("pts"),
            P("pts"),
            P(),
            P(),
            P(),
            P(None, None, "ch"),
            P(),
            P(None, "ch"),
        ),
        out_specs=(P("pts", "ch"), P("pts", "ch")),
        check_vma=False,
    )
```

profile of v0, /device:TPU:1, one launch (start us, length us, event | category | flops | bytes accessed | tf_op | source)
XLA Modules:
  0.0 208.8 jit_solution(9440661710691054107)
XLA Ops:
  0.7 0.9 fusion.87
  1.6 4.6 %collective-permute-start = (bf16[128,256]{1,0:T(8,128)(2,1)S(1)}, bf16[128,256]{1,0:T(8,128)(2,1)S(1)}, u32[]{:S(2)}, u32[]{:S(2)}) collective-permute-start(bf16[128,256]{1,0:T(8,128)(2,1)S(1)} %get-tuple-element.46), channel_id=1, source_target_pairs={{0,4},{4,8},{8,12},{12,16},{16,20},{20,24},{24,28},{28,32},{32,36}... | collective-permute-start | bytes 196616 | tf_op jit(solution)/shard_map/ppermute | solution.py:19
  6.2 5.5 %collective-permute-start.1 = (bf16[128,256]{1,0:T(8,128)(2,1)S(1)}, bf16[128,256]{1,0:T(8,128)(2,1)S(1)}, u32[]{:S(2)}, u32[]{:S(2)}) collective-permute-start(bf16[128,256]{1,0:T(8,128)(2,1)S(1)} %get-tuple-element.45), channel_id=1, source_target_pairs={{4,0},{8,4},{12,8},{16,12},{20,16},{24,20},{28,24},{32,28},{36,32}... | collective-permute-start | bytes 196616 | tf_op jit(solution)/shard_map/ppermute | solution.py:20
  12.8 0.9 convert_reduce_fusion.1
  14.4 15.8 %all-to-all-start.1 = ((s32[128,1,1]{2,1,0:T(1,128)}), s32[128,1,1]{2,1,0:T(1,128)S(1)}, u32[]{:S(2)}, u32[]{:S(2)}) async-start(s32[128,1,1]{2,1,0:T(1,128)} %copy.107), calls=%async_computation.1 | async-start | bytes 131072 | tf_op jit(solution)/shard_map/all_to_all | solution.py:122
  30.2 1.8 copy.85
  32.0 1.2 compare_select_fusion.15
  33.2 1.1 fusion.88
  34.3 1.1 fusion.33
  35.4 1.1 fusion.34
  36.5 1.1 fusion.35
  37.5 1.1 fusion.36
  38.6 1.1 fusion.37
  39.7 1.9 fusion.38
  41.5 1.9 fusion.39
  43.4 1.9 fusion.40
  45.3 1.9 fusion.41
  47.1 1.9 fusion.42
  49.0 1.9 fusion.43
  50.9 1.1 fusion.44
  52.0 1.2 fusion.45
  53.2 1.2 fusion.46
  54.3 1.2 fusion.47
  55.5 1.1 fusion.48
  60.9 2.1 %gather_fusion.14 = bf16[512,256]{1,0:T(8,128)(2,1)S(1)} fusion(bf16[768,256]{1,0:T(8,128)(2,1)S(1)} %constant_dynamic-update-slice_fusion, s32[1024]{0:T(1024)} %get-tuple-element.82), kind=kCustom, calls=%fused_computation.14 | custom fusion | bytes 526336 | tf_op jit(solution)/shard_map/gather | solution.py:94
  63.9 2.2 %gather_fusion.15 = bf16[512,256]{1,0:T(8,128)(2,1)S(1)} fusion(bf16[768,256]{1,0:T(8,128)(2,1)S(1)} %constant_dynamic-update-slice_fusion, s32[1024]{0:T(1024)} %get-tuple-element.81), kind=kCustom, calls=%fused_computation.15 | custom fusion | bytes 526336 | tf_op jit(solution)/shard_map/gather | solution.py:94
  67.0 2.2 %gather_fusion = bf16[512,256]{1,0:T(8,128)(2,1)S(1)} fusion(bf16[768,256]{1,0:T(8,128)(2,1)S(1)} %constant_dynamic-update-slice_fusion, s32[1024]{0:T(1024)} %get-tuple-element.96), kind=kCustom, calls=%fused_computation | custom fusion | bytes 526336 | tf_op jit(solution)/shard_map/gather | solution.py:94
  70.0 1.9 gather_fusion.1
  72.9 1.9 gather_fusion.2
  75.7 1.9 gather_fusion.3
  78.5 1.9 gather_fusion.4
  81.3 1.9 gather_fusion.5
  84.1 1.9 gather_fusion.6
  86.9 2.1 %gather_fusion.7 = bf16[512,256]{1,0:T(8,128)(2,1)S(1)} fusion(bf16[768,256]{1,0:T(8,128)(2,1)S(1)} %constant_dynamic-update-slice_fusion, s32[1024]{0:T(1024)S(1)} %copy-done.7), kind=kCustom, calls=%fused_computation.7 | custom fusion | bytes 526336 | tf_op jit(solution)/shard_map/gather | solution.py:94
  89.8 1.9 gather_fusion.8
  92.6 1.9 gather_fusion.9
  95.4 1.9 gather_fusion.10
  98.2 1.9 gather_fusion.11
  100.2 0.9 copy.97
  101.1 1.9 gather_fusion.12
  103.9 1.9 gather_fusion.13
  106.0 5.0 %convert_reduce_fusion = (f32[512]{0:T(512)S(1)}, bf16[512,256]{0,1:T(8,128)(2,1)S(1)}) fusion(f32[512,256]{0,1:T(8,128)} %fusion.48, bf16[512,256]{0,1:T(8,128)(2,1)} %copy.101, f32[512,256]{0,1:T(8,128)} %fusion.47, bf16[512,256]{0,1:T(8,128)(2,1)} %copy.100, f32[512,256]{0,1:T(8,128)} %fusion.46, bf16[512,256]{0,1:T(8,128)(2,1)S(1)} %copy.99, ...), kind=kLoop, calls=%fused_computation.34 | loop fusion | flops 6815232 | bytes 13109248 | tf_op jit(solution)/shard_map/reduce_sum | solution.py:98
  111.6 2.5 %scatter_custom_fusion = bf16[1024,192]{1,0:T(8,128)(2,1)S(1)} fusion(s32[512]{0:T(512)S(1)} %copy-done.14, bf16[512,192]{1,0:T(8,128)(2,1)S(1)} %copy.104, bf16[]{:T(256)} %constant.131.clone.1), kind=kCustom, calls=%fused_computation.54 | custom fusion | bytes 393218 | tf_op jit(solution)/shard_map/scatter | solution.py:117
  115.3 3.0 %reduce.7 = bf16[128,1536]{1,0:T(8,128)(2,1)S(1)} reduce(bf16[128,1,1536]{2,1,0:T(2,128)(2,1)S(1)} %all_to_all.24, bf16[]{:T(256)} %broadcast.271), dimensions={1}, to_apply=%all_to_all.24.reduce_sub_computation | reduce | bytes 786434 | tf_op jit(solution)/shard_map/all_to_all | solution.py:121
  119.2 14.1 %all-to-all-start = ((bf16[128,2,768]{2,1,0:T(2,128)(2,1)}), bf16[128,2,768]{2,1,0:T(2,128)(2,1)S(1)}, u32[]{:S(2)}, u32[]{:S(2)}) async-start(bf16[128,2,768]{2,1,0:T(2,128)(2,1)} %reshape.325), calls=%async_computation | async-start | bytes 786432 | tf_op jit(solution)/shard_map/all_to_all | solution.py:121
  133.3 2.4 %reduce.5 = s32[128]{0:T(128)S(1)} reduce(s32[128,1,1]{2,1,0:T(1,128)S(1)} %all-to-all-done.1, s32[]{:T(128)} %constant.129.clone.1), dimensions={1,2}, to_apply=%all_to_all.21.reduce_sub_computation | reduce | bytes 1028 | tf_op jit(solution)/shard_map/all_to_all | solution.py:122
  135.8 15.2 %all-to-all-done = bf16[128,2,768]{2,1,0:T(2,128)(2,1)S(1)} async-done(((bf16[128,2,768]{2,1,0:T(2,128)(2,1)}), bf16[128,2,768]{2,1,0:T(2,128)(2,1)S(1)}, u32[]{:S(2)}, u32[]{:S(2)}) %all-to-all-start) | async-done | bytes 393248 | tf_op jit(solution)/shard_map/all_to_all | solution.py:121
  151.3 2.4 %reduce.4 = bf16[128,1536]{1,0:T(8,128)(2,1)S(1)} reduce(bf16[128,1,1536]{2,1,0:T(2,128)(2,1)S(1)} %reshape.326, bf16[]{:T(256)} %constant.176), dimensions={1}, to_apply=%all_to_all.19.reduce_sub_computation | reduce | bytes 786434 | tf_op jit(solution)/shard_map/all_to_all | solution.py:121
  153.7 1.0 squeeze.15
  154.7 1.1 fusion.86
  156.9 1.7 fusion
  158.6 2.4 %fusion.1 = f32[2,1024]{1,0:T(2,128)S(1)} fusion(f32[2,1024,1024]{1,2,0:T(8,128)S(1)} %get-tuple-element.80, f32[2,1024]{1,0:T(2,128)S(1)} %get-tuple-element.79, pred[1024]{0:T(1024)(128)(4,1)S(1)} %lt.115), kind=kLoop, calls=%fused_computation.23 | loop fusion | flops 8386560 | bytes 8406016 | tf_op jit(solution)/shard_map/while/body/eval_jaxpr/reduce_sum | solution.py:52
  161.0 1.9 fusion.13
  163.9 1.4 reduce.8
  166.0 5.5 %all-to-all-start.2 = ((bf16[128,2,256]{2,1,0:T(2,128)(2,1)}), bf16[128,2,256]{2,1,0:T(2,128)(2,1)S(1)}, u32[]{:S(2)}, u32[]{:S(2)}) async-start(bf16[128,2,256]{2,1,0:T(2,128)(2,1)} %reshape.327), calls=%async_computation.2 | async-start | bytes 262144 | tf_op jit(solution)/shard_map/all_to_all | solution.py:129
  171.5 4.1 %scatter_custom_fusion.2 = f32[129]{0:T(256)S(1)} fusion(s32[512]{0:T(512)S(1)} %subtract_add_fusion, f32[512]{0:T(512)S(1)} %broadcast.149, f32[]{:T(128)} %constant.134.clone.1), kind=kCustom, calls=%fused_computation.176 | custom fusion | flops 512 | bytes 520 | tf_op jit(solution)/shard_map/scatter-add | solution.py:148
  176.1 2.9 %collective-permute-start.3 = (f32[1]{0:T(128)}, f32[1]{0:T(128)}, u32[]{:S(2)}, u32[]{:S(2)}) collective-permute-start(f32[1]{0:T(128)} %slice.207), channel_id=1, source_target_pairs={{4,0},{8,4},{12,8},{16,12},{20,16},{24,20},{28,24},{32,28},{36,32}... | collective-permute-start | bytes 20 | tf_op jit(solution)/shard_map/ppermute | solution.py:28
  179.1 2.0 collective-permute-done.3
  181.7 2.6 %all-to-all-done.2 = bf16[128,2,256]{2,1,0:T(2,128)(2,1)S(1)} async-done(((bf16[128,2,256]{2,1,0:T(2,128)(2,1)}), bf16[128,2,256]{2,1,0:T(2,128)(2,1)S(1)}, u32[]{:S(2)}, u32[]{:S(2)}) %all-to-all-start.2) | async-done | bytes 131104 | tf_op jit(solution)/shard_map/all_to_all | solution.py:129
  185.3 1.3 gather_fusion.16
  186.8 10.2 %all-gather = bf16[512,256]{0,1:T(8,128)(2,1)S(1)} all-gather(bf16[512,64]{0,1:T(8,128)(2,1)S(1)} %copy.113), channel_id=2, replica_groups=mesh['pts'=128,'ch'=4] {'ch'}, dimensions={1}, use_global_device_ids=true | all-gather | bytes 327680 | tf_op jit(solution)/shard_map/all_gather | solution.py:138
  197.5 3.5 %scatter_custom_fusion.1 = f32[129,128]{1,0:T(8,128)S(1)} fusion(s32[512]{0:T(512)S(1)} %subtract_add_fusion, f32[512,128]{1,0:T(8,128)S(1)} %fusion.89, f32[]{:T(128)} %constant.134.clone.1), kind=kCustom, calls=%fused_computation.130 | custom fusion | flops 65536 | bytes 66052 | tf_op jit(solution)/shard_map/scatter-add | solution.py:147
  201.0 4.7 %collective-permute-start.2 = (f32[1,128]{1,0:T(1,128)S(1)}, f32[1,128]{1,0:T(1,128)S(1)}, u32[]{:S(2)}, u32[]{:S(2)}) collective-permute-start(f32[1,128]{1,0:T(1,128)S(1)} %slice.248), channel_id=1, source_target_pairs={{4,0},{8,4},{12,8},{16,12},{20,16},{24,20},{28,24},{32,28},{36,32}... | collective-permute-start | bytes 1544 | tf_op jit(solution)/shard_map/ppermute | solution.py:28
  206.4 1.0 collective-permute-done.2
  (112 shorter events, 28.4 us)
Async XLA Ops:
  0.6 196.4 %copy-start = (bf16[256,256]{1,0:T(8,128)(2,1)S(1)}, bf16[256,256]{1,0:T(8,128)(2,1)}, u32[]{:S(2)}) copy-start(bf16[256,256]{1,0:T(8,128)(2,1)} %param.24) | copy-start | bytes 393220
  0.6 56.0 %copy-start.4 = (s32[512]{0:T(512)S(1)}, s32[512]{0:T(512)}, u32[]{:S(2)}) copy-start(s32[512]{0:T(512)} %param.19) | copy-start | bytes 6148
  0.7 50.2 %copy-start.1 = (bf16[27,256]{1,0:T(8,128)(2,1)S(1)}, bf16[27,256]{1,0:T(8,128)(2,1)}, u32[]{:S(2)}) copy-start(bf16[27,256]{1,0:T(8,128)(2,1)} %param.20) | copy-start | bytes 41476
  1.6 59.2 %collective-permute-start = (bf16[128,256]{1,0:T(8,128)(2,1)S(1)}, bf16[128,256]{1,0:T(8,128)(2,1)S(1)}, u32[]{:S(2)}, u32[]{:S(2)}) collective-permute-start(bf16[128,256]{1,0:T(8,128)(2,1)S(1)} %get-tuple-element.46), channel_id=1, source_target_pairs={{0,4},{4,8},{8,12},{12,16},{16,20},{20,24},{24,28},{28,32},{32,36}... | collective-permute-start | bytes 196616 | tf_op jit(solution)/shard_map/ppermute | solution.py:19
  6.2 54.7 %collective-permute-start.1 = (bf16[128,256]{1,0:T(8,128)(2,1)S(1)}, bf16[128,256]{1,0:T(8,128)(2,1)S(1)}, u32[]{:S(2)}, u32[]{:S(2)}) collective-permute-start(bf16[128,256]{1,0:T(8,128)(2,1)S(1)} %get-tuple-element.45), channel_id=1, source_target_pairs={{4,0},{8,4},{12,8},{16,12},{20,16},{24,20},{28,24},{32,28},{36,32}... | collective-permute-start | bytes 196616 | tf_op jit(solution)/shard_map/ppermute | solution.py:20
  14.4 104.8 %all-to-all-start.1 = ((s32[128,1,1]{2,1,0:T(1,128)}), s32[128,1,1]{2,1,0:T(1,128)S(1)}, u32[]{:S(2)}, u32[]{:S(2)}) async-start(s32[128,1,1]{2,1,0:T(1,128)} %copy.107), calls=%async_computation.1 | async-start | bytes 131072 | tf_op jit(solution)/shard_map/all_to_all | solution.py:122
  32.0 28.8 %copy-start.2 = (bf16[512,256]{1,0:T(8,128)(2,1)S(1)}, bf16[512,256]{1,0:T(8,128)(2,1)}, u32[]{:S(2)}) copy-start(bf16[512,256]{1,0:T(8,128)(2,1)} %param.15) | copy-start | bytes 786436
  60.9 9.2 %copy-start.13 = (s32[1024]{0:T(1024)S(1)}, s32[1024]{0:T(1024)}, u32[]{:S(2)}) copy-start(s32[1024]{0:T(1024)} %get-tuple-element.95) | copy-start | bytes 12292
  60.9 12.0 %copy-start.12 = (s32[1024]{0:T(1024)S(1)}, s32[1024]{0:T(1024)}, u32[]{:S(2)}) copy-start(s32[1024]{0:T(1024)} %get-tuple-element.94) | copy-start | bytes 12292
  60.9 14.8 %copy-start.11 = (s32[1024]{0:T(1024)S(1)}, s32[1024]{0:T(1024)}, u32[]{:S(2)}) copy-start(s32[1024]{0:T(1024)} %get-tuple-element.93) | copy-start | bytes 12292
  60.9 17.5 %copy-start.10 = (s32[1024]{0:T(1024)S(1)}, s32[1024]{0:T(1024)}, u32[]{:S(2)}) copy-start(s32[1024]{0:T(1024)} %get-tuple-element.92) | copy-start | bytes 12292
  63.9 17.4 %copy-start.9 = (s32[1024]{0:T(1024)S(1)}, s32[1024]{0:T(1024)}, u32[]{:S(2)}) copy-start(s32[1024]{0:T(1024)} %get-tuple-element.91) | copy-start | bytes 12292
  67.0 17.1 %copy-start.8 = (s32[1024]{0:T(1024)S(1)}, s32[1024]{0:T(1024)}, u32[]{:S(2)}) copy-start(s32[1024]{0:T(1024)} %get-tuple-element.90) | copy-start | bytes 12292
  70.0 16.8 %copy-start.7 = (s32[1024]{0:T(1024)S(1)}, s32[1024]{0:T(1024)}, u32[]{:S(2)}) copy-start(s32[1024]{0:T(1024)} %get-tuple-element.89) | copy-start | bytes 12292
  72.8 17.0 %copy-start.6 = (s32[1024]{0:T(1024)S(1)}, s32[1024]{0:T(1024)}, u32[]{:S(2)}) copy-start(s32[1024]{0:T(1024)} %get-tuple-element.88) | copy-start | bytes 12292
  75.7 17.0 %copy-start.5 = (s32[1024]{0:T(1024)S(1)}, s32[1024]{0:T(1024)}, u32[]{:S(2)}) copy-start(s32[1024]{0:T(1024)} %get-tuple-element.87) | copy-start | bytes 12292
  103.0 8.1 %copy-start.17 = (f32[256]{0:T(256)S(1)}, f32[256]{0:T(256)}, u32[]{:S(2)}) copy-start(f32[256]{0:T(256)} %param.22) | copy-start | bytes 3076
  103.0 8.1 %copy-start.18 = (f32[256]{0:T(256)S(1)}, f32[256]{0:T(256)}, u32[]{:S(2)}) copy-start(f32[256]{0:T(256)} %param.21) | copy-start | bytes 3076
  105.9 5.3 %copy-start.16 = (bf16[3,256,64]{1,2,0:T(8,128)(2,1)S(1)}, bf16[3,256,64]{1,2,0:T(8,128)(2,1)}, u32[]{:S(2)}) copy-start(bf16[3,256,64]{1,2,0:T(8,128)(2,1)} %param.23) | copy-start | bytes 294916
  105.9 5.7 %copy-start.14 = (s32[512]{0:T(512)S(1)}, s32[512]{0:T(512)}, u32[]{:S(2)}) copy-start(s32[512]{0:T(512)} %compare_select_fusion.16) | copy-start | bytes 6148
  119.2 31.8 %all-to-all-start = ((bf16[128,2,768]{2,1,0:T(2,128)(2,1)}), bf16[128,2,768]{2,1,0:T(2,128)(2,1)S(1)}, u32[]{:S(2)}, u32[]{:S(2)}) async-start(bf16[128,2,768]{2,1,0:T(2,128)(2,1)} %reshape.325), calls=%async_computation | async-start | bytes 786432 | tf_op jit(solution)/shard_map/all_to_all | solution.py:121
  161.0 10.5 %copy-start.15 = (s32[512]{0:T(512)S(1)}, s32[512]{0:T(512)}, u32[]{:S(2)}) copy-start(s32[512]{0:T(512)} %param.18) | copy-start | bytes 6148
  161.0 36.3 %copy-start.3 = (bf16[256,128]{1,0:T(8,128)(2,1)S(1)}, bf16[256,128]{1,0:T(8,128)(2,1)}, u32[]{:S(2)}) copy-start(bf16[256,128]{1,0:T(8,128)(2,1)} %param.25) | copy-start | bytes 196612
  166.0 18.3 %all-to-all-start.2 = ((bf16[128,2,256]{2,1,0:T(2,128)(2,1)}), bf16[128,2,256]{2,1,0:T(2,128)(2,1)S(1)}, u32[]{:S(2)}, u32[]{:S(2)}) async-start(bf16[128,2,256]{2,1,0:T(2,128)(2,1)} %reshape.327), calls=%async_computation.2 | async-start | bytes 262144 | tf_op jit(solution)/shard_map/all_to_all | solution.py:129
  176.1 5.0 %collective-permute-start.3 = (f32[1]{0:T(128)}, f32[1]{0:T(128)}, u32[]{:S(2)}, u32[]{:S(2)}) collective-permute-start(f32[1]{0:T(128)} %slice.207), channel_id=1, source_target_pairs={{4,0},{8,4},{12,8},{16,12},{20,16},{24,20},{28,24},{32,28},{36,32}... | collective-permute-start | bytes 20 | tf_op jit(solution)/shard_map/ppermute | solution.py:28
  201.0 6.4 %collective-permute-start.2 = (f32[1,128]{1,0:T(1,128)S(1)}, f32[1,128]{1,0:T(1,128)S(1)}, u32[]{:S(2)}, u32[]{:S(2)}) collective-permute-start(f32[1,128]{1,0:T(1,128)S(1)} %slice.248), channel_id=1, source_target_pairs={{4,0},{8,4},{12,8},{16,12},{20,16},{24,20},{28,24},{32,28},{36,32}... | collective-permute-start | bytes 1544 | tf_op jit(solution)/shard_map/ppermute | solution.py:28
where the time goes:
time: 213 us; the launch traced here: 209 us
  local copies, waits for them, and re-layouts  63.2 us (30%)
  starting transfers between devices  52.9 us (25%)
  other arithmetic  33.1 us (16%)
  matrix products  26.8 us (13%)
  waiting for transfers between devices  20.8 us (10%)
  blocking collectives  10.2 us (5%)
    gather x32, local copies, waits for them, and re-layouts, shards(): picked = padded[offsets_base + neighbor_offsets[:, neighbor_slot]]  44.9 us
    dot_general x16, matrix products, shards(): jnp.dot(selector, conv_weight, preferred_element_type=jnp.float32)  22.3 us
    all_to_all x1, starting transfers between devices, shards(): lax.all_to_all(send_counts, 'pts', split_axis=0, concat_axis=0, tiled=True)  15.8 us
    all_to_all x1, waiting for transfers between devices, shards(): lax.all_to_all(outgoing, 'pts', split_axis=0, concat_axis=0, tiled=True)  15.2 us
    all_to_all x1, starting transfers between devices, shards(): lax.all_to_all(outgoing, 'pts', split_axis=0, concat_axis=0, tiled=True)  14.1 us
    all_gather x1, blocking collectives, shards(): lax.all_gather(returned, 'ch', axis=1, tiled=True)  10.2 us
    ppermute x2, starting transfers between devices, from_behind(): return lax.ppermute(value, axis, pairs)  7.61 us
    ppermute x1, starting transfers between devices, padded_2(): after = lax.ppermute(initial, axis, down)  5.46 us
  transfers between devices with their start and end apart: 7, of which 4 were waited for; matrix products, arithmetic and copies ran while one was open for 47% of the time, Pallas kernels for 0%

commit v1 on v0

--- a/solution.py
+++ b/solution.py
@@ -1,3 +1,4 @@
+import functools
 import math
 import jax
 import jax.numpy as jnp
@@ -7,6 +8,16 @@
 HD = 32
 PATCH = 1024
 G = 128
+
+
+def fit_the_sums_all(load, dim_i):
+    current_value = lax.axis_size("ch")
+    reply = jnp.stack([load] * current_value)
+    prior = lax.all_to_all(reply, axis_name="ch", split_axis=0, concat_axis=0)
+    return jnp.concatenate(prior, dim_i)
+
+
+spread_surface = functools.partial(fit_the_sums_all, dim_i=1)
 
 
 def padded_2(value, sides, width):
@@ -135,9 +146,7 @@
     )
     returned = returned_rows.reshape(slot_total, head_cols)[position]
     projected_sum = jnp.dot(
-        lax.all_gather(returned, "ch", axis=1, tiled=True),
-        proj_weight,
-        preferred_element_type=jnp.float32,
+        spread_surface(returned), proj_weight, preferred_element_type=jnp.float32
     )
     full_out = (residual_rows.astype(jnp.float32) + projected_sum).astype(jnp.bfloat16)
     block_out = lax.dynamic_slice_in_dim(full_out, channel_index * head_cols, head_cols, 1)

time: 213 us -> 229 us (1.075)
  local copies, waits for them, and re-layouts: 63.2 us -> 75.7 us
  waiting for transfers between devices: 20.8 us -> 32.6 us
  blocking collectives: 10.2 us -> 0 us
    gather x32, local copies, waits for them, and re-layouts: 44.9 us -> 55.1 us  [shards(): picked = padded[offsets_base + neighbor_offsets[:, neighbor_slot]]]
    all_to_all x1, waiting for transfers between devices: 2.58 us -> 12.8 us  [shards(): lax.all_to_all(attended.reshape(node_count, capacity * head_cols), 'pts',...]
    all_gather x1 -> x0, blocking collectives: 10.2 us -> none  [shards(): lax.all_gather(returned, 'ch', axis=1, tiled=True)]
    all_to_all x0 -> x1, starting transfers between devices: none -> 4.01 us  [fit_the_sums_all(): prior = lax.all_to_all(reply, axis_name='ch', split_axis=0, concat_axis=0)]
    ppermute x2, starting transfers between devices: 7.61 us -> 4.49 us  [from_behind(): return lax.ppermute(value, axis, pairs)]
    unnamed x49 -> x51, local copies, waits for them, and re-layouts: 4.92 us -> 5.78 us
  transfers between devices with their start and end apart: 7 -> 8, of which waited for: 4 -> 4; matrix products, arithmetic and copies ran while one was open for 47% -> 49% of each run, Pallas kernels for 0% -> 0%
where the time goes in v1:
time: 229 us; the launch traced here: 224 us
  local copies, waits for them, and re-layouts  75.7 us (33%)
  starting transfers between devices  53.8 us (23%)
  other arithmetic  33.6 us (15%)
  waiting for transfers between devices  32.6 us (14%)
  matrix products  26.7 us (12%)
    gather x32, local copies, waits for them, and re-layouts, shards(): picked = padded[offsets_base + neighbor_offsets[:, neighbor_slot]]  55.1 us
    dot_general x16, matrix products, shards(): jnp.dot(selector, conv_weight, preferred_element_type=jnp.float32)  22.2 us
    all_to_all x1, waiting for transfers between devices, shards(): lax.all_to_all(outgoing, 'pts', split_axis=0, concat_axis=0, tiled=True)  15.2 us
    all_to_all x1, starting transfers between devices, shards(): lax.all_to_all(send_counts, 'pts', split_axis=0, concat_axis=0, tiled=True)  15.2 us
    all_to_all x1, starting transfers between devices, shards(): lax.all_to_all(outgoing, 'pts', split_axis=0, concat_axis=0, tiled=True)  14.1 us
    all_to_all x1, waiting for transfers between devices, shards(): lax.all_to_all(attended.reshape(node_count, capacity * head_cols), 'pts',...  12.8 us
    ppermute x1, starting transfers between devices, padded_2(): after = lax.ppermute(initial, axis, down)  6.06 us
    unnamed x51, local copies, waits for them, and re-layouts  5.78 us
  transfers between devices with their start and end apart: 8, of which 4 were waited for; matrix products, arithmetic and copies ran while one was open for 49% of the time, Pallas kernels for 0%

profile of v1, /device:TPU:1, one launch (start us, length us, event | category | flops | bytes accessed | tf_op | source)
XLA Modules:
  0.0 224.1 jit_solution(16524759333036613918)
XLA Ops:
  0.7 1.6 fusion.87
  2.3 4.6 %collective-permute-start = (bf16[128,256]{1,0:T(8,128)(2,1)}, bf16[128,256]{1,0:T(8,128)(2,1)}, u32[]{:S(2)}, u32[]{:S(2)}) collective-permute-start(bf16[128,256]{1,0:T(8,128)(2,1)} %get-tuple-element.46), channel_id=1, source_target_pairs={{0,4},{4,8},{8,12},{12,16},{16,20},{20,24},{24,28},{28,32},{32,36}... | collective-permute-start | bytes 196616 | tf_op jit(solution)/shard_map/ppermute | solution.py:30
  6.8 6.1 %collective-permute-start.1 = (bf16[128,256]{1,0:T(8,128)(2,1)}, bf16[128,256]{1,0:T(8,128)(2,1)S(1)}, u32[]{:S(2)}, u32[]{:S(2)}) collective-permute-start(bf16[128,256]{1,0:T(8,128)(2,1)} %get-tuple-element.45), channel_id=1, source_target_pairs={{4,0},{8,4},{12,8},{16,12},{20,16},{24,20},{28,24},{32,28},{36,32}... | collective-permute-start | bytes 196616 | tf_op jit(solution)/shard_map/ppermute | solution.py:31
  15.7 15.2 %all-to-all-start.1 = ((s32[128,1,1]{2,1,0:T(1,128)}), s32[128,1,1]{2,1,0:T(1,128)S(1)}, u32[]{:S(2)}, u32[]{:S(2)}) async-start(s32[128,1,1]{2,1,0:T(1,128)} %copy.108), calls=%async_computation.1 | async-start | bytes 131072 | tf_op jit(solution)/shard_map/all_to_all | solution.py:133
  30.9 1.8 copy.86
  32.7 1.1 compare_select_fusion.15
  33.8 1.1 fusion.88
  34.9 1.1 fusion.33
  35.9 1.1 fusion.34
  40.2 1.9 fusion.38
  42.1 1.9 fusion.39
  44.0 1.9 fusion.40
  45.8 1.9 fusion.41
  47.7 1.9 fusion.42
  49.5 1.9 fusion.43
  51.4 1.1 fusion.44
  52.6 1.2 fusion.45
  53.7 1.2 fusion.46
  54.9 1.2 fusion.47
  56.0 1.1 fusion.48
  62.8 2.1 gather_fusion.13
  65.8 2.2 gather_fusion.14
  68.9 2.2 gather_fusion.15
  72.0 1.9 gather_fusion
  74.8 1.9 gather_fusion.1
  77.6 1.9 gather_fusion.2
  80.4 1.9 gather_fusion.3
  83.2 1.9 gather_fusion.4
  86.0 1.9 gather_fusion.5
  88.8 2.1 gather_fusion.6
  91.8 2.6 %gather_fusion.7 = bf16[512,256]{1,0:T(8,128)(2,1)} fusion(bf16[768,256]{1,0:T(8,128)(2,1)S(1)} %constant_dynamic-update-slice_fusion, s32[1024]{0:T(1024)S(1)} %copy-done.7), kind=kCustom, calls=%fused_computation.7 | custom fusion | bytes 526336 | tf_op jit(solution)/shard_map/gather | solution.py:105
  94.4 1.8 copy.94
  96.2 2.6 %gather_fusion.8 = bf16[512,256]{1,0:T(8,128)(2,1)} fusion(bf16[768,256]{1,0:T(8,128)(2,1)S(1)} %constant_dynamic-update-slice_fusion, s32[1024]{0:T(1024)S(1)} %copy-done.6), kind=kCustom, calls=%fused_computation.8 | custom fusion | bytes 526336 | tf_op jit(solution)/shard_map/gather | solution.py:105
  98.8 1.8 copy.95
  100.6 2.6 %gather_fusion.9 = bf16[512,256]{1,0:T(8,128)(2,1)} fusion(bf16[768,256]{1,0:T(8,128)(2,1)S(1)} %constant_dynamic-update-slice_fusion, s32[1024]{0:T(1024)S(1)} %get-tuple-element.87), kind=kCustom, calls=%fused_computation.9 | custom fusion | bytes 526336 | tf_op jit(solution)/shard_map/gather | solution.py:105
  103.1 1.8 copy.96
  105.0 2.6 %gather_fusion.10 = bf16[512,256]{1,0:T(8,128)(2,1)} fusion(bf16[768,256]{1,0:T(8,128)(2,1)S(1)} %constant_dynamic-update-slice_fusion, s32[1024]{0:T(1024)S(1)} %get-tuple-element.86), kind=kCustom, calls=%fused_computation.10 | custom fusion | bytes 526336 | tf_op jit(solution)/shard_map/gather | solution.py:105
  107.5 1.8 copy.97
  109.3 2.6 %gather_fusion.11 = bf16[512,256]{1,0:T(8,128)(2,1)} fusion(bf16[768,256]{1,0:T(8,128)(2,1)S(1)} %constant_dynamic-update-slice_fusion, s32[1024]{0:T(1024)S(1)} %get-tuple-element.85), kind=kCustom, calls=%fused_computation.11 | custom fusion | bytes 526336 | tf_op jit(solution)/shard_map/gather | solution.py:105
  111.9 1.8 copy.98
  113.7 2.6 %gather_fusion.12 = bf16[512,256]{1,0:T(8,128)(2,1)} fusion(bf16[768,256]{1,0:T(8,128)(2,1)S(1)} %constant_dynamic-update-slice_fusion, s32[1024]{0:T(1024)S(1)} %get-tuple-element.84), kind=kCustom, calls=%fused_computation.12 | custom fusion | bytes 526336 | tf_op jit(solution)/shard_map/gather | solution.py:105
  116.3 1.8 copy.99
  118.1 4.9 %convert_reduce_fusion = (f32[512]{0:T(512)S(1)}, bf16[512,256]{0,1:T(8,128)(2,1)S(1)}) fusion(f32[512,256]{0,1:T(8,128)} %fusion.48, bf16[512,256]{0,1:T(8,128)(2,1)} %copy.102, f32[512,256]{0,1:T(8,128)} %fusion.47, bf16[512,256]{0,1:T(8,128)(2,1)} %copy.101, f32[512,256]{0,1:T(8,128)} %fusion.46, bf16[512,256]{0,1:T(8,128)(2,1)} %copy.100, ...), kind=kLoop, calls=%fused_computation.34 | loop fusion | flops 6815232 | bytes 13109248 | tf_op jit(solution)/shard_map/reduce_sum | solution.py:109
  123.7 2.5 %scatter_custom_fusion = bf16[1024,192]{1,0:T(8,128)(2,1)S(1)} fusion(s32[512]{0:T(512)S(1)} %copy-done.15, bf16[512,192]{1,0:T(8,128)(2,1)S(1)} %copy.105, bf16[]{:T(256)} %constant.131.clone.1), kind=kCustom, calls=%fused_computation.54 | custom fusion | bytes 393218 | tf_op jit(solution)/shard_map/scatter | solution.py:128
  127.4 3.0 %reduce.7 = bf16[128,1536]{1,0:T(8,128)(2,1)S(1)} reduce(bf16[128,1,1536]{2,1,0:T(2,128)(2,1)S(1)} %all_to_all.28, bf16[]{:T(256)} %broadcast.273), dimensions={1}, to_apply=%all_to_all.28.reduce_sub_computation | reduce | bytes 786434 | tf_op jit(solution)/shard_map/all_to_all | solution.py:132
  131.2 14.1 %all-to-all-start = ((bf16[128,2,768]{2,1,0:T(2,128)(2,1)}), bf16[128,2,768]{2,1,0:T(2,128)(2,1)S(1)}, u32[]{:S(2)}, u32[]{:S(2)}) async-start(bf16[128,2,768]{2,1,0:T(2,128)(2,1)} %reshape.334), calls=%async_computation | async-start | bytes 786432 | tf_op jit(solution)/shard_map/all_to_all | solution.py:132
  145.3 2.4 %reduce.5 = s32[128]{0:T(128)S(1)} reduce(s32[128,1,1]{2,1,0:T(1,128)S(1)} %all-to-all-done.1, s32[]{:T(128)} %constant.129.clone.1), dimensions={1,2}, to_apply=%all_to_all.24.reduce_sub_computation | reduce | bytes 1028 | tf_op jit(solution)/shard_map/all_to_all | solution.py:133
  147.9 15.2 %all-to-all-done = bf16[128,2,768]{2,1,0:T(2,128)(2,1)S(1)} async-done(((bf16[128,2,768]{2,1,0:T(2,128)(2,1)}), bf16[128,2,768]{2,1,0:T(2,128)(2,1)S(1)}, u32[]{:S(2)}, u32[]{:S(2)}) %all-to-all-start) | async-done | bytes 393248 | tf_op jit(solution)/shard_map/all_to_all | solution.py:132
  163.4 2.4 %reduce.4 = bf16[128,1536]{1,0:T(8,128)(2,1)S(1)} reduce(bf16[128,1,1536]{2,1,0:T(2,128)(2,1)S(1)} %reshape.335, bf16[]{:T(256)} %constant.176), dimensions={1}, to_apply=%all_to_all.22.reduce_sub_computation | reduce | bytes 786434 | tf_op jit(solution)/shard_map/all_to_all | solution.py:132
  166.7 1.1 fusion.86
  168.9 1.7 fusion
  170.6 2.4 %fusion.1 = f32[2,1024]{1,0:T(2,128)S(1)} fusion(f32[2,1024,1024]{1,2,0:T(8,128)S(1)} %get-tuple-element.80, f32[2,1024]{1,0:T(2,128)S(1)} %get-tuple-element.79, pred[1024]{0:T(1024)(128)(4,1)S(1)} %lt.115), kind=kLoop, calls=%fused_computation.23 | loop fusion | flops 8386560 | bytes 8406016 | tf_op jit(solution)/shard_map/while/body/eval_jaxpr/reduce_sum | solution.py:63
  173.1 1.9 fusion.13
  176.0 1.4 reduce.8
  178.1 5.4 %all-to-all-start.2 = ((bf16[128,2,256]{2,1,0:T(2,128)(2,1)}), bf16[128,2,256]{2,1,0:T(2,128)(2,1)S(1)}, u32[]{:S(2)}, u32[]{:S(2)}) async-start(bf16[128,2,256]{2,1,0:T(2,128)(2,1)} %reshape.336), calls=%async_computation.2 | async-start | bytes 262144 | tf_op jit(solution)/shard_map/all_to_all | solution.py:140
  183.5 12.8 %all-to-all-done.2 = bf16[128,2,256]{2,1,0:T(2,128)(2,1)S(1)} async-done(((bf16[128,2,256]{2,1,0:T(2,128)(2,1)}), bf16[128,2,256]{2,1,0:T(2,128)(2,1)S(1)}, u32[]{:S(2)}, u32[]{:S(2)}) %all-to-all-start.2) | async-done | bytes 131104 | tf_op jit(solution)/shard_map/all_to_all | solution.py:140
  197.4 1.3 gather_fusion.16
  199.5 4.0 %all-to-all-start.3 = ((bf16[4,512,64]{1,2,0:T(8,128)(2,1)}), bf16[4,512,64]{1,2,0:T(8,128)(2,1)S(1)}, u32[]{:S(2)}, u32[]{:S(2)}) async-start(bf16[4,512,64]{1,2,0:T(8,128)(2,1)} %stack.2), calls=%async_computation.3 | async-start | bytes 524288 | tf_op jit(solution)/shard_map/all_to_all | solution.py:16
  203.6 4.1 %scatter_custom_fusion.2 = f32[129]{0:T(256)S(1)} fusion(s32[512]{0:T(512)S(1)} %subtract_add_fusion, f32[512]{0:T(512)S(1)} %broadcast.151, f32[]{:T(128)} %constant.134.clone.1), kind=kCustom, calls=%fused_computation.176 | custom fusion | flops 512 | bytes 520 | tf_op jit(solution)/shard_map/scatter-add | solution.py:157
  208.2 2.6 %collective-permute-start.3 = (f32[1]{0:T(128)}, f32[1]{0:T(128)}, u32[]{:S(2)}, u32[]{:S(2)}) collective-permute-start(f32[1]{0:T(128)} %slice.207), channel_id=1, source_target_pairs={{4,0},{8,4},{12,8},{16,12},{20,16},{24,20},{28,24},{32,28},{36,32}... | collective-permute-start | bytes 20 | tf_op jit(solution)/shard_map/ppermute | solution.py:39
  210.8 2.3 %collective-permute-done.3 = f32[1]{0:T(128)} collective-permute-done((f32[1]{0:T(128)}, f32[1]{0:T(128)}, u32[]{:S(2)}, u32[]{:S(2)}) %collective-permute-start.3) | collective-permute-done | bytes 36 | tf_op jit(solution)/shard_map/ppermute | solution.py:39
  214.4 3.5 %scatter_custom_fusion.1 = f32[129,128]{1,0:T(8,128)S(1)} fusion(s32[512]{0:T(512)S(1)} %subtract_add_fusion, f32[512,128]{1,0:T(8,128)S(1)} %fusion.89, f32[]{:T(128)} %constant.134.clone.1), kind=kCustom, calls=%fused_computation.130 | custom fusion | flops 65536 | bytes 66052 | tf_op jit(solution)/shard_map/scatter-add | solution.py:156
  217.9 1.9 collective-permute-start.2
  220.5 2.3 %collective-permute-done.2 = f32[1,128]{1,0:T(1,128)S(1)} collective-permute-done((f32[1,128]{1,0:T(1,128)S(1)}, f32[1,128]{1,0:T(1,128)S(1)}, u32[]{:S(2)}, u32[]{:S(2)}) %collective-permute-start.2) | collective-permute-done | bytes 544 | tf_op jit(solution)/shard_map/ppermute | solution.py:39
  (116 shorter events, 32.2 us)
Async XLA Ops:
  0.6 213.2 %copy-start = (bf16[256,256]{1,0:T(8,128)(2,1)S(1)}, bf16[256,256]{1,0:T(8,128)(2,1)}, u32[]{:S(2)}) copy-start(bf16[256,256]{1,0:T(8,128)(2,1)} %param.24) | copy-start | bytes 393220
  0.6 62.1 %copy-start.2 = (bf16[512,256]{1,0:T(8,128)(2,1)S(1)}, bf16[512,256]{1,0:T(8,128)(2,1)}, u32[]{:S(2)}) copy-start(bf16[512,256]{1,0:T(8,128)(2,1)} %param.15) | copy-start | bytes 786436
  0.7 56.5 %copy-start.5 = (s32[512]{0:T(512)S(1)}, s32[512]{0:T(512)}, u32[]{:S(2)}) copy-start(s32[512]{0:T(512)} %param.19) | copy-start | bytes 6148
  0.7 50.7 %copy-start.1 = (bf16[27,256]{1,0:T(8,128)(2,1)S(1)}, bf16[27,256]{1,0:T(8,128)(2,1)}, u32[]{:S(2)}) copy-start(bf16[27,256]{1,0:T(8,128)(2,1)} %param.20) | copy-start | bytes 41476
  2.3 59.6 %collective-permute-start = (bf16[128,256]{1,0:T(8,128)(2,1)}, bf16[128,256]{1,0:T(8,128)(2,1)}, u32[]{:S(2)}, u32[]{:S(2)}) collective-permute-start(bf16[128,256]{1,0:T(8,128)(2,1)} %get-tuple-element.46), channel_id=1, source_target_pairs={{0,4},{4,8},{8,12},{12,16},{16,20},{20,24},{24,28},{28,32},{32,36}... | collective-permute-start | bytes 196616 | tf_op jit(solution)/shard_map/ppermute | solution.py:30
  6.8 55.9 %collective-permute-start.1 = (bf16[128,256]{1,0:T(8,128)(2,1)}, bf16[128,256]{1,0:T(8,128)(2,1)S(1)}, u32[]{:S(2)}, u32[]{:S(2)}) collective-permute-start(bf16[128,256]{1,0:T(8,128)(2,1)} %get-tuple-element.45), channel_id=1, source_target_pairs={{4,0},{8,4},{12,8},{16,12},{20,16},{24,20},{28,24},{32,28},{36,32}... | collective-permute-start | bytes 196616 | tf_op jit(solution)/shard_map/ppermute | solution.py:31
  15.7 115.6 %all-to-all-start.1 = ((s32[128,1,1]{2,1,0:T(1,128)}), s32[128,1,1]{2,1,0:T(1,128)S(1)}, u32[]{:S(2)}, u32[]{:S(2)}) async-start(s32[128,1,1]{2,1,0:T(1,128)} %copy.108), calls=%async_computation.1 | async-start | bytes 131072 | tf_op jit(solution)/shard_map/all_to_all | solution.py:133
  62.8 9.2 %copy-start.14 = (s32[1024]{0:T(1024)S(1)}, s32[1024]{0:T(1024)}, u32[]{:S(2)}) copy-start(s32[1024]{0:T(1024)} %get-tuple-element.96) | copy-start | bytes 12292
  62.8 12.0 %copy-start.13 = (s32[1024]{0:T(1024)S(1)}, s32[1024]{0:T(1024)}, u32[]{:S(2)}) copy-start(s32[1024]{0:T(1024)} %get-tuple-element.95) | copy-start | bytes 12292
  62.8 14.8 %copy-start.12 = (s32[1024]{0:T(1024)S(1)}, s32[1024]{0:T(1024)}, u32[]{:S(2)}) copy-start(s32[1024]{0:T(1024)} %get-tuple-element.94) | copy-start | bytes 12292
  62.8 17.6 %copy-start.11 = (s32[1024]{0:T(1024)S(1)}, s32[1024]{0:T(1024)}, u32[]{:S(2)}) copy-start(s32[1024]{0:T(1024)} %get-tuple-element.93) | copy-start | bytes 12292
  65.8 17.4 %copy-start.10 = (s32[1024]{0:T(1024)S(1)}, s32[1024]{0:T(1024)}, u32[]{:S(2)}) copy-start(s32[1024]{0:T(1024)} %get-tuple-element.92) | copy-start | bytes 12292
  68.9 17.1 %copy-start.9 = (s32[1024]{0:T(1024)S(1)}, s32[1024]{0:T(1024)}, u32[]{:S(2)}) copy-start(s32[1024]{0:T(1024)} %get-tuple-element.91) | copy-start | bytes 12292
  72.0 16.9 %copy-start.8 = (s32[1024]{0:T(1024)S(1)}, s32[1024]{0:T(1024)}, u32[]{:S(2)}) copy-start(s32[1024]{0:T(1024)} %get-tuple-element.90) | copy-start | bytes 12292
  74.8 17.0 %copy-start.7 = (s32[1024]{0:T(1024)S(1)}, s32[1024]{0:T(1024)}, u32[]{:S(2)}) copy-start(s32[1024]{0:T(1024)} %get-tuple-element.89) | copy-start | bytes 12292
  77.6 18.6 %copy-start.6 = (s32[1024]{0:T(1024)S(1)}, s32[1024]{0:T(1024)}, u32[]{:S(2)}) copy-start(s32[1024]{0:T(1024)} %get-tuple-element.88) | copy-start | bytes 12292
  91.8 26.3 %copy-start.3 = (bf16[512,256]{0,1:T(8,128)(2,1)S(1)}, bf16[512,256]{0,1:T(8,128)(2,1)}, u32[]{:S(2)}) copy-start(bf16[512,256]{0,1:T(8,128)(2,1)} %copy.86) | copy-start | bytes 786436
  111.9 11.3 %copy-start.18 = (f32[256]{0:T(256)S(1)}, f32[256]{0:T(256)}, u32[]{:S(2)}) copy-start(f32[256]{0:T(256)} %param.22) | copy-start | bytes 3076
  111.9 11.3 %copy-start.19 = (f32[256]{0:T(256)S(1)}, f32[256]{0:T(256)}, u32[]{:S(2)}) copy-start(f32[256]{0:T(256)} %param.21) | copy-start | bytes 3076
  116.3 7.4 %copy-start.15 = (s32[512]{0:T(512)S(1)}, s32[512]{0:T(512)}, u32[]{:S(2)}) copy-start(s32[512]{0:T(512)} %compare_select_fusion.16) | copy-start | bytes 6148
  118.1 5.1 %copy-start.17 = (bf16[3,256,64]{1,2,0:T(8,128)(2,1)S(1)}, bf16[3,256,64]{1,2,0:T(8,128)(2,1)}, u32[]{:S(2)}) copy-start(bf16[3,256,64]{1,2,0:T(8,128)(2,1)} %param.23) | copy-start | bytes 294916
  131.2 31.8 %all-to-all-start = ((bf16[128,2,768]{2,1,0:T(2,128)(2,1)}), bf16[128,2,768]{2,1,0:T(2,128)(2,1)S(1)}, u32[]{:S(2)}, u32[]{:S(2)}) async-start(bf16[128,2,768]{2,1,0:T(2,128)(2,1)} %reshape.334), calls=%async_computation | async-start | bytes 786432 | tf_op jit(solution)/shard_map/all_to_all | solution.py:132
  173.0 30.5 %copy-start.16 = (s32[512]{0:T(512)S(1)}, s32[512]{0:T(512)}, u32[]{:S(2)}) copy-start(s32[512]{0:T(512)} %param.18) | copy-start | bytes 6148
  173.1 41.1 %copy-start.4 = (bf16[256,128]{1,0:T(8,128)(2,1)S(1)}, bf16[256,128]{1,0:T(8,128)(2,1)}, u32[]{:S(2)}) copy-start(bf16[256,128]{1,0:T(8,128)(2,1)} %param.25) | copy-start | bytes 196612
  178.1 18.3 %all-to-all-start.2 = ((bf16[128,2,256]{2,1,0:T(2,128)(2,1)}), bf16[128,2,256]{2,1,0:T(2,128)(2,1)S(1)}, u32[]{:S(2)}, u32[]{:S(2)}) async-start(bf16[128,2,256]{2,1,0:T(2,128)(2,1)} %reshape.336), calls=%async_computation.2 | async-start | bytes 262144 | tf_op jit(solution)/shard_map/all_to_all | solution.py:140
  199.5 14.3 %all-to-all-start.3 = ((bf16[4,512,64]{1,2,0:T(8,128)(2,1)}), bf16[4,512,64]{1,2,0:T(8,128)(2,1)S(1)}, u32[]{:S(2)}, u32[]{:S(2)}) async-start(bf16[4,512,64]{1,2,0:T(8,128)(2,1)} %stack.2), calls=%async_computation.3 | async-start | bytes 524288 | tf_op jit(solution)/shard_map/all_to_all | solution.py:16
  208.2 5.0 %collective-permute-start.3 = (f32[1]{0:T(128)}, f32[1]{0:T(128)}, u32[]{:S(2)}, u32[]{:S(2)}) collective-permute-start(f32[1]{0:T(128)} %slice.207), channel_id=1, source_target_pairs={{4,0},{8,4},{12,8},{16,12},{20,16},{24,20},{28,24},{32,28},{36,32}... | collective-permute-start | bytes 20 | tf_op jit(solution)/shard_map/ppermute | solution.py:39
  217.9 4.9 %collective-permute-start.2 = (f32[1,128]{1,0:T(1,128)S(1)}, f32[1,128]{1,0:T(1,128)S(1)}, u32[]{:S(2)}, u32[]{:S(2)}) collective-permute-start(f32[1,128]{1,0:T(1,128)S(1)} %slice.248), channel_id=1, source_target_pairs={{4,0},{8,4},{12,8},{16,12},{20,16},{24,20},{28,24},{32,28},{36,32}... | collective-permute-start | bytes 1544 | tf_op jit(solution)/shard_map/ppermute | solution.py:39
